TPU v7x, 128 devices: a whole 4x4x4 slice. The times are simulated.
128 devices in a mesh: grp: 2 (over z_hi), pix: 64 (over x, y, z_lo, core).
Axes of the slice: x: 4, y: 4, z: 4 (z_hi: 2, z_lo: 2; z = z_hi * 2 + z_lo), core: 2. Of those that a mesh axis runs over, the one named last changes fastest.
Arguments:
- fields: bfloat16 [2, 2, 128, 512, 512], P('grp', None, None, 'pix'), may hold values from -6 to 6
- lens_phase: float32 [512, 512], P('pix'), may hold values from -3.140625 to 3.140625
- occupancy: float32 [256], replicated, may hold values from 0.05 to 1
- focus_scale: float32 [256], replicated, may hold values from 0.5 to 1.5
- assignment: int32 [256], replicated, may hold values from 0 to 255, each once
- start_basis: float32 [2, 256, 128], replicated, may hold values from -6 to 6
Outputs:
- coherent_modes: bfloat16 [2, 128, 512, 512], P(None, None, 'pix', 'grp')
- relative_power: float32 [128], replicated
Inputs may be any that keep to these rules, and one draw needn't show every extreme that they name: `assignment`: each electron is carried by exactly one wavefront slot.
All inputs are finite; a program needn't handle non-finite values.
Results may differ from a plain program's by a relative error of at most 0.0018.
The roundings to bfloat16 on the way count: a program that leaves them out, or rounds other values in their place, can miss the bound.
Values may be sent and summed in bfloat16 or wider, within the bound.
No kernel may reach another device: no remote copies, remote signals or barrier semaphores. Data moves between devices by JAX's collectives and lax.ppermute only.
A program may use at most 64 MiB of HBM per device.

v0:
```python
import math
import jax
import jax.numpy as jnp
from jax import lax
from jax.sharding import PartitionSpec as P

NROW = 512
NCOL = 512
STEPS = 2


def partner_2(array, axis, apart):
    return lax.ppermute(array, axis, [(i, i ^ 1 << apart) for i in range(lax.axis_size(axis))])


def dft_tables(length):
    index = jnp.arange(length, dtype=jnp.int32)
    product = index[:, None] * index[None, :] % length
    angle = product.astype(jnp.float32) * (2.0 * math.pi / length)
    factor = 1.0 / math.sqrt(length)
    return (
        (jnp.cos(angle) * factor).astype(jnp.bfloat16),
        (jnp.sin(angle) * factor).astype(jnp.bfloat16),
    )


def local(fields, lens_phase, occupancy, focus_scale, assignment, start_basis):
    highest = lax.Precision.HIGHEST
    local_fields = fields[0]
    modes = local_fields.shape[1]
    group_index = lax.axis_index("grp")
    electron = lax.dynamic_slice_in_dim(assignment, group_index * modes, modes)
    choose = (
        electron[:, None] == jnp.arange(assignment.shape[0], dtype=jnp.int32)[None, :]
    ).astype(jnp.float32)
    amplitude = jnp.sqrt(jnp.sum(choose * occupancy[None, :], axis=1))[:, None, None]
    chromatic = jnp.sum(choose * focus_scale[None, :], axis=1)
    angle = chromatic[:, None, None] * lens_phase[None]
    cosine = jnp.cos(angle)
    sine = jnp.sin(angle)
    field_re = local_fields[0].astype(jnp.float32)
    field_im = local_fields[1].astype(jnp.float32)
    phased = jnp.stack(
        [
            amplitude * (field_re * cosine - field_im * sine),
            amplitude * (field_re * sine + field_im * cosine),
        ]
    ).astype(jnp.bfloat16)
    cos_cols, sin_cols = dft_tables(lens_phase.shape[1])
    col_cos = jnp.einsum("zmrc,ck->zmkr", phased, cos_cols, preferred_element_type=jnp.float32)
    col_sin = jnp.einsum("zmrc,ck->zmkr", phased, sin_cols, preferred_element_type=jnp.float32)
    across = jnp.stack([col_cos[0] + col_sin[1], col_cos[1] - col_sin[0]]).astype(jnp.bfloat16)
    full_rows = across.shape[3] * lax.axis_size("pix")
    cos_rows, sin_rows = dft_tables(full_rows)
    pieces = lax.all_to_all(across, "pix", split_axis=2, concat_axis=3, tiled=True)
    row_cos = jnp.dot(pieces, cos_rows, preferred_element_type=jnp.float32)
    row_sin = jnp.dot(pieces, sin_rows, preferred_element_type=jnp.float32)
    focal = jnp.stack([row_cos[0] + row_sin[1], row_cos[1] - row_sin[0]]).astype(jnp.bfloat16)
    stack_size = modes * lax.axis_size("grp")
    half_rows = full_rows // lax.axis_size("grp")
    partner = partner_2(focal, "grp", 0)
    leading = jnp.where(group_index == 0, focal, partner)
    trailing = jnp.where(group_index == 0, partner, focal)
    stacked = jnp.concatenate([leading, trailing], axis=1)
    flat = stacked.reshape(2, stack_size, -1)
    blocks = jnp.einsum("xap,ybp->xyab", flat, flat, preferred_element_type=jnp.float32)
    local_re = blocks[0, 0] + blocks[1, 1]
    local_im = blocks[0, 1] - blocks[1, 0]
    gram_re, gram_im = lax.psum((local_re, local_im), "pix")
    owned = lax.dynamic_slice_in_dim(stacked, group_index * half_rows, half_rows, 3)
    basis_re = start_basis[0]
    basis_im = start_basis[1]
    for iteration in range(STEPS):
        image_re = jnp.dot(gram_re, basis_re, precision=highest) - jnp.dot(
            gram_im, basis_im, precision=highest
        )
        image_im = jnp.dot(gram_re, basis_im, precision=highest) + jnp.dot(
            gram_im, basis_re, precision=highest
        )
        column_norm = jnp.sqrt(jnp.sum(image_re * image_re + image_im * image_im, axis=0) + 1e-06)
        basis_re = image_re / column_norm[None, :]
        basis_im = image_im / column_norm[None, :]
    rounded = jnp.stack([basis_re, basis_im]).astype(jnp.bfloat16)
    rank = rounded.shape[2]
    owned_flat = owned.reshape(2, stack_size, -1)
    products = jnp.einsum("xsk,ysp->xykp", rounded, owned_flat, preferred_element_type=jnp.float32)
    mode_re = products[0, 0] - products[1, 1]
    mode_im = products[0, 1] + products[1, 0]
    energy = lax.psum(jnp.sum(mode_re * mode_re + mode_im * mode_im, axis=1), ("grp", "pix"))
    trace = jnp.sum(jnp.diagonal(gram_re))
    relative_power = energy * stack_size / trace
    inverse = lax.rsqrt(energy / (NROW * NCOL) + 1e-06)
    coherent_modes = (jnp.stack([mode_re, mode_im]) * inverse[None, :, None]).astype(jnp.bfloat16)
    return (coherent_modes.reshape(2, rank, owned.shape[2], owned.shape[3]), relative_power)


def solution(mesh):
    in_specs = (P("grp", None, None, "pix", None), P("pix", None), P(), P(), P(), P())
    out_specs = (P(None, None, "pix", "grp"), P())
    return jax.shard_map(local, mesh=mesh, in_specs=in_specs, out_specs=out_specs, check_vma=False)
```

profile of v0, /device:TPU:1, one launch (start us, length us, event | category | flops | bytes accessed | tf_op | source)
XLA Modules:
  0.0 779.3 jit_solution(8011462047435173882)
XLA Ops:
  7.2 0.8 dynamic_slice.6
  8.0 0.9 select_reduce_fusion.1
  8.9 1.7 fusion.84
  10.6 9.2 %fusion.9 = (bf16[1,128,8,512]{3,1,2,0:T(8,128)(2,1)S(1)}, bf16[1,128,8,512]{3,1,2,0:T(8,128)(2,1)S(1)}) fusion(f32[8,512]{1,0:T(8,128)S(1)} %copy-done.5, f32[128]{0:T(128)S(1)} %get-tuple-element.3, f32[128]{0:T(128)S(1)} %sqrt.21, bf16[1,1,128,8,512]{4,3,2,1,0:T(8,128)(2,1)S(1)} %get-tuple-element.18, bf16[1,1,128,8,512]{4,3,2,1,0:T(8,128)(2,1)S(1)} %get-tuple-element.17), kind=kLoop, calls=%fused_computation.18 | loop fusion | flops 6815744 | bytes 4211712 | tf_op jit(solution)/shard_map/convert.10
  19.8 4.9 convolution_bitcast_fusion.2
  24.7 5.0 convolution_bitcast_fusion.1
  30.4 1.5 copy.51
  31.9 39.1 %all_to_all.18 = bf16[2,128,512,8]{1,3,0,2:T(8,128)(2,1)S(1)} all-to-all(bf16[2,128,512,8]{1,3,0,2:T(8,128)(2,1)S(1)} %copy.51), channel_id=1, replica_groups=mesh['grp'=2,'pix'=64] {'pix'}, dimensions={2} | all-to-all | bytes 4194304 | tf_op jit(solution)/shard_map/all_to_all | solution.py:55
  71.0 4.8 fusion.19
  75.8 4.8 fusion.21
  80.6 1.3 fusion.15
  81.8 1.5 pad_maximum_fusion.4
  83.4 3.6 collective-permute-start
  86.9 46.2 %collective-permute-done = bf16[2,128,8,512]{3,1,2,0:T(8,128)(2,1)} collective-permute-done((bf16[2,128,8,512]{3,1,2,0:T(8,128)(2,1)}, bf16[2,128,8,512]{3,1,2,0:T(8,128)(2,1)}, u32[]{:S(2)}, u32[]{:S(2)}) %collective-permute-start) | collective-permute-done | bytes 2097184 | tf_op jit(solution)/shard_map/ppermute | solution.py:13
  133.2 1.9 broadcast_select_fusion
  135.0 2.4 fusion.25
  137.4 0.9 fusion.42
  138.4 3.1 fusion.13
  141.5 2.9 copy.56
  144.4 544.8 %all-reduce.3.cloned.1.call-done = (f32[256,256]{0,1:T(8,128)}, f32[256,256]{0,1:T(8,128)}) async-done(((f32[256,256]{0,1:T(8,128)}, f32[256,256]{0,1:T(8,128)}), (f32[256,256]{0,1:T(8,128)}, f32[256,256]{0,1:T(8,128)})) %all-reduce.3.cloned.1.call-update) | async-done | bytes 524304 | tf_op jit(solution)/shard_map/psum | solution.py:69
  689.2 1.6 fusion.50
  690.8 1.5 fusion.46
  692.3 1.5 convolution_subtract_fusion.1
  693.9 1.6 add_reduce_fusion.2
  696.6 0.6 convolution_subtract_fusion
  697.2 0.6 add_reduce_fusion.1
  697.9 0.7 convolution_bitcast_fusion
  698.9 67.0 %psum.23 = f32[128]{0:T(128)S(1)} all-reduce(f32[128]{0:T(128)S(1)} %get-tuple-element.6), channel_id=1, replica_groups=mesh['grp'=2,'pix'=64] {'grp','pix'}, use_global_device_ids=true, to_apply=%region_7.8 | all-reduce | flops 128 | bytes 1024 | tf_op jit(solution)/shard_map/psum | solution.py:89
  766.0 2.4 gather_fusion
  769.3 0.6 reduce_sum.59
  769.9 1.2 multiply_divide_fusion
  771.1 1.2 fusion.18
  (26 shorter events, 3.3 us)
Async XLA Ops:
  7.2 682.0 %all-reduce.3.cloned.1.call-start = ((), (), s32[]{:S(2)}) async-start(), calls=%async_computation.1 | async-start | bytes 1048576 | tf_op jit(solution)/shard_map/psum | solution.py:69
  8.9 1.7 copy-start.5
  83.4 49.8 %collective-permute-start = (bf16[2,128,8,512]{3,1,2,0:T(8,128)(2,1)}, bf16[2,128,8,512]{3,1,2,0:T(8,128)(2,1)}, u32[]{:S(2)}, u32[]{:S(2)}) collective-permute-start(bf16[2,128,8,512]{3,1,2,0:T(8,128)(2,1)} %pad_maximum_fusion.4), channel_id=1, source_target_pairs={{0,64},{64,0},{1,65},{65,1},{2,66},{66,2},{3,67},{67,3},{4,68},{68... | collective-permute-start | bytes 6291464 | tf_op jit(solution)/shard_map/ppermute | solution.py:13
  135.0 2.4 copy-start.1
  135.0 2.4 copy-start.2
  141.5 547.7 %copy-start.4 = (f32[2,256,128]{2,1,0:T(8,128)S(1)}, f32[2,256,128]{2,1,0:T(8,128)}, u32[]{:S(2)}) copy-start(f32[2,256,128]{2,1,0:T(8,128)} %param.11) | copy-start | bytes 786436
  689.1 6.3 copy-start
  689.1 7.5 copy-start.3
Sparse Core Ops, SparseCore 0:
  138.5 550.6 all-reduce.2
where the time goes:
time: 782 us; the launch traced here: 779 us
  waiting for transfers between devices  591 us (76%)
  blocking collectives  106 us (14%)
  matrix products  31.2 us (4%)
  other arithmetic  22.7 us (3%)
  between operations  14.5 us (2%)
  local copies, waits for them, and re-layouts  10.2 us (1%)
    psum x1, waiting for transfers between devices, local(): gram_re, gram_im = lax.psum((local_re, local_im), 'pix')  545 us
    psum x1, blocking collectives, local(): lax.psum(jnp.sum(mode_re * mode_re + mode_im * mode_im, axis=1), ('grp',...  67 us
    ppermute x1, waiting for transfers between devices, partner_2(): lax.ppermute(array, axis, [(i, i ^ 1 << apart) for i in range(lax.axis_si...  46.2 us
    all_to_all x1, blocking collectives, local(): lax.all_to_all(across, 'pix', split_axis=2, concat_axis=3, tiled=True)  39.1 us
  transfers between devices with their start and end apart: 2, of which 2 were waited for; matrix products, arithmetic and copies ran while one was open for 1% of the time, Pallas kernels for 0%

commit v1 on v0

--- a/solution.py
+++ b/solution.py
@@ -7,6 +7,11 @@
 NROW = 512
 NCOL = 512
 STEPS = 2
+
+
+def gather_and_add(value, axis):
+    pieces = lax.all_gather(value, axis)
+    return jnp.sum(pieces, axis=0)
 
 
 def partner_2(array, axis, apart):
@@ -86,7 +91,7 @@
     products = jnp.einsum("xsk,ysp->xykp", rounded, owned_flat, preferred_element_type=jnp.float32)
     mode_re = products[0, 0] - products[1, 1]
     mode_im = products[0, 1] + products[1, 0]
-    energy = lax.psum(jnp.sum(mode_re * mode_re + mode_im * mode_im, axis=1), ("grp", "pix"))
+    energy = gather_and_add(jnp.sum(mode_re * mode_re + mode_im * mode_im, axis=1), ("grp", "pix"))
     trace = jnp.sum(jnp.diagonal(gram_re))
     relative_power = energy * stack_size / trace
     inverse = lax.rsqrt(energy / (NROW * NCOL) + 1e-06)

time: 782 us -> 893 us (1.14)
  blocking collectives: 106 us -> 216 us
    all_gather x0 -> x1, blocking collectives: none -> 177 us  [gather_and_add(): pieces = lax.all_gather(value, axis)]
    psum x1 -> x0, blocking collectives: 67 us -> none  [local(): lax.psum(jnp.sum(mode_re * mode_re + mode_im * mode_im, axis=1), ('grp',...]
where the time goes in v1:
time: 893 us; the launch traced here: 890 us
  waiting for transfers between devices  591 us (66%)
  blocking collectives  216 us (24%)
  matrix products  31.2 us (3%)
  other arithmetic  22.8 us (3%)
  between operations  14.5 us (2%)
  local copies, waits for them, and re-layouts  10.2 us (1%)
    psum x1, waiting for transfers between devices, local(): gram_re, gram_im = lax.psum((local_re, local_im), 'pix')  545 us
    all_gather x1, blocking collectives, gather_and_add(): pieces = lax.all_gather(value, axis)  177 us
    ppermute x1, waiting for transfers between devices, partner_2(): lax.ppermute(array, axis, [(i, i ^ 1 << apart) for i in range(lax.axis_si...  46.2 us
    all_to_all x1, blocking collectives, local(): lax.all_to_all(across, 'pix', split_axis=2, concat_axis=3, tiled=True)  39.1 us
  transfers between devices with their start and end apart: 2, of which 2 were waited for; matrix products, arithmetic and copies ran while one was open for 1% of the time, Pallas kernels for 0%

profile of v1, /device:TPU:1, one launch (start us, length us, event | category | flops | bytes accessed | tf_op | source)
XLA Modules:
  0.0 889.7 jit_solution(17494671391567531645)
XLA Ops:
  7.2 0.8 dynamic_slice.6
  8.0 0.9 select_reduce_fusion.1
  8.9 1.7 fusion.84
  10.6 9.2 %fusion.9 = (bf16[1,128,8,512]{3,1,2,0:T(8,128)(2,1)S(1)}, bf16[1,128,8,512]{3,1,2,0:T(8,128)(2,1)S(1)}) fusion(f32[8,512]{1,0:T(8,128)S(1)} %copy-done.5, f32[128]{0:T(128)S(1)} %get-tuple-element.3, f32[128]{0:T(128)S(1)} %sqrt.21, bf16[1,1,128,8,512]{4,3,2,1,0:T(8,128)(2,1)S(1)} %get-tuple-element.18, bf16[1,1,128,8,512]{4,3,2,1,0:T(8,128)(2,1)S(1)} %get-tuple-element.17), kind=kLoop, calls=%fused_computation.18 | loop fusion | flops 6815744 | bytes 4211712 | tf_op jit(solution)/shard_map/convert.10
  19.8 4.9 convolution_bitcast_fusion.2
  24.7 5.0 convolution_bitcast_fusion.1
  30.4 1.5 copy.51
  31.9 39.1 %all_to_all.18 = bf16[2,128,512,8]{1,3,0,2:T(8,128)(2,1)S(1)} all-to-all(bf16[2,128,512,8]{1,3,0,2:T(8,128)(2,1)S(1)} %copy.51), channel_id=1, replica_groups=mesh['grp'=2,'pix'=64] {'pix'}, dimensions={2} | all-to-all | bytes 4194304 | tf_op jit(solution)/shard_map/all_to_all | solution.py:60
  71.0 4.8 fusion.19
  75.8 4.8 fusion.21
  80.6 1.3 fusion.15
  81.8 1.5 pad_maximum_fusion.4
  83.4 3.6 collective-permute-start
  86.9 46.2 %collective-permute-done = bf16[2,128,8,512]{3,1,2,0:T(8,128)(2,1)} collective-permute-done((bf16[2,128,8,512]{3,1,2,0:T(8,128)(2,1)}, bf16[2,128,8,512]{3,1,2,0:T(8,128)(2,1)}, u32[]{:S(2)}, u32[]{:S(2)}) %collective-permute-start) | collective-permute-done | bytes 2097184 | tf_op jit(solution)/shard_map/ppermute | solution.py:18
  133.2 1.9 broadcast_select_fusion
  135.0 2.4 fusion.25
  137.4 0.9 fusion.42
  138.4 3.1 fusion.13
  141.5 2.9 copy.56
  144.4 544.8 %all-reduce.3.cloned.1.call-done = (f32[256,256]{0,1:T(8,128)}, f32[256,256]{0,1:T(8,128)}) async-done(((f32[256,256]{0,1:T(8,128)}, f32[256,256]{0,1:T(8,128)}), (f32[256,256]{0,1:T(8,128)}, f32[256,256]{0,1:T(8,128)})) %all-reduce.3.cloned.1.call-update) | async-done | bytes 524304 | tf_op jit(solution)/shard_map/psum | solution.py:74
  689.2 1.6 fusion.50
  690.8 1.5 fusion.46
  692.3 1.5 convolution_subtract_fusion.1
  693.9 1.6 add_reduce_fusion.2
  696.6 0.6 convolution_subtract_fusion
  697.2 0.6 add_reduce_fusion.1
  697.9 0.7 convolution_bitcast_fusion
  698.9 177.2 %all-gather.1 = f32[128,1,128]{2,1,0:T(1,128)S(1)} all-gather(f32[1,1,128]{2,1,0:T(1,128)S(1)} %bitcast.105), channel_id=2, replica_groups=mesh['grp'=2,'pix'=64] {'grp','pix'}, dimensions={0}, use_global_device_ids=true | all-gather | bytes 66048 | tf_op jit(solution)/shard_map/all_gather | solution.py:13
  876.2 2.4 gather_fusion
  878.7 0.6 reduce_sum.69
  880.3 1.2 multiply_divide_fusion
  881.4 1.2 fusion.18
  (27 shorter events, 3.4 us)
Async XLA Ops:
  7.2 682.0 %all-reduce.3.cloned.1.call-start = ((), (), s32[]{:S(2)}) async-start(), calls=%async_computation.1 | async-start | bytes 1048576 | tf_op jit(solution)/shard_map/psum | solution.py:74
  8.9 1.7 copy-start.5
  83.4 49.8 %collective-permute-start = (bf16[2,128,8,512]{3,1,2,0:T(8,128)(2,1)}, bf16[2,128,8,512]{3,1,2,0:T(8,128)(2,1)}, u32[]{:S(2)}, u32[]{:S(2)}) collective-permute-start(bf16[2,128,8,512]{3,1,2,0:T(8,128)(2,1)} %pad_maximum_fusion.4), channel_id=1, source_target_pairs={{0,64},{64,0},{1,65},{65,1},{2,66},{66,2},{3,67},{67,3},{4,68},{68... | collective-permute-start | bytes 6291464 | tf_op jit(solution)/shard_map/ppermute | solution.py:18
  135.0 2.4 copy-start.1
  135.0 2.4 copy-start.2
  141.5 547.7 %copy-start.4 = (f32[2,256,128]{2,1,0:T(8,128)S(1)}, f32[2,256,128]{2,1,0:T(8,128)}, u32[]{:S(2)}) copy-start(f32[2,256,128]{2,1,0:T(8,128)} %param.11) | copy-start | bytes 786436
  689.1 6.3 copy-start
  689.1 7.5 copy-start.3
Sparse Core Ops, SparseCore 0:
  138.5 550.6 all-reduce.2
